TPU v7x, 512 devices: a whole 4x8x8 slice. The times are simulated.
512 devices in a mesh: tile: 128 (over x, z, y_lo), spec: 4 (over y_hi, core).
Axes of the slice: x: 4, y: 8 (y_hi: 2, y_lo: 4; y = y_hi * 4 + y_lo), z: 8, core: 2. Of those that a mesh axis runs over, the one named last changes fastest.
Arguments:
- adjoint: float32 [128, 8, 512, 128], P('spec', None, 'tile'), may hold values from -6 to 6
- section_first: bfloat16 [128, 8, 128, 128], P('tile'), may hold values from -1 to 2
- section_second: bfloat16 [128, 8, 128, 128], P('tile'), may hold values from -1 to 2
- jacobian: bfloat16 [128, 8, 128, 128], P('tile'), may hold values from -0.5 to 0.5
- pattern: int32 [128, 8, 2, 2], P('tile'), may hold values 0 or 1
- counts: int32 [128, 8], P('tile'), may hold values from 1 to 512, as said below
- courant: float32 [8, 512, 128], P(None, 'tile'), may hold values from -0.45 to 0.45
- seam_codes: int32 [128, 2], P('tile'), may hold values from 0 to 1, as said below
Outputs:
- adjoint_out: float32 [128, 8, 512, 128], P('spec', None, 'tile')
Inputs may be any that keep to these rules, and one draw needn't show every extreme that they name: The active cells of tile t and level l are the first counts[t, l] of its 4 x 128 cells in row-major order. `seam_codes`: column 0 of tile t is the code of the seam between tile t and tile t + 1, column 1 that of the seam between tile t - 1 and tile t (cyclically); a 1 means that the seam reverses the order of cells along it. `pattern`: 1 where a block is present.
All inputs are finite; a program needn't handle non-finite values.
Results may differ from a plain program's by a relative error of at most 0.004.
Values may be sent and summed in bfloat16 or wider, within the bound.
No kernel may reach another device: no remote copies, remote signals or barrier semaphores. Data moves between devices by JAX's collectives and lax.ppermute only.
A program may use at most 64 MiB of HBM per device.

v0:
```python
import jax
import jax.numpy as jnp
from jax import lax
from jax.sharding import PartitionSpec as P

NSUB = 4
section_weights = (0.4, 0.3, 0.2, 0.1)
coupling = 0.5


def passed_along(value, axis, steps):
    count = lax.axis_size(axis)
    pairs = [(source, (source + steps) % count) for source in range(count)]
    return lax.ppermute(value, axis, pairs)


def padded(block, sides, width):
    for axis, dim in sides:
        count = lax.axis_size(axis)
        forward = [(i, i + 1) for i in range(count - 1)]
        forward.append((count - 1, 0))
        backward = [(target, source) for source, target in forward]
        low = lax.ppermute(
            lax.slice_in_dim(block, block.shape[dim] - width, None, axis=dim), axis, forward
        )
        high = lax.ppermute(lax.slice_in_dim(block, 0, width, axis=dim), axis, backward)
        block = jnp.concatenate([low, block, high], axis=dim)
    return block


def transposed(matrix, field_cells):
    return jnp.einsum("lsp,slc->plc", matrix, field_cells, preferred_element_type=jnp.float32)


def section_chain(rounded, first_factor, second_factor, jac_used, offset, out_width):
    start_wide = rounded.astype(jnp.float32)
    first_y = transposed(first_factor, rounded).astype(jnp.bfloat16)
    section_u = transposed(second_factor, first_y).astype(jnp.bfloat16)
    running_sum = None
    for section in range(4):
        if section < 3:
            coupled = transposed(jac_used, section_u)
            picked = lax.dynamic_slice_in_dim(coupled, offset, out_width, 0)
        else:
            picked = transposed(lax.dynamic_slice_in_dim(jac_used, offset, out_width, 2), section_u)
        if section == 0:
            running_sum = section_weights[0] * picked
        else:
            running_sum = running_sum + section_weights[section] * picked
        if section < 3:
            mixed_term = (start_wide + coupling * coupled).astype(jnp.bfloat16)
            first_y = transposed(first_factor, mixed_term).astype(jnp.bfloat16)
            section_u = transposed(second_factor, first_y).astype(jnp.bfloat16)
    return running_sum.astype(jnp.bfloat16)


def reorder(rim_cells, seam_code):
    return jnp.where(seam_code == 1, jnp.flip(rim_cells, axis=-1), rim_cells)


def shards(adjoint, section_first, section_second, jacobian, pattern, counts, courant, seam_codes):
    species_dev, levels, rows_dev, seam_len = adjoint.shape
    species_all = jacobian.shape[2]
    block_size = species_all // pattern.shape[2]
    cell_count = rows_dev * seam_len
    first_factor = section_first[0]
    second_factor = section_second[0]
    present = jnp.repeat(jnp.repeat(pattern[0], block_size, axis=1), block_size, axis=2) == 1
    jac_used = jnp.where(present, jacobian[0], jnp.zeros_like(jacobian[0]))
    own_part = adjoint.astype(jnp.bfloat16).reshape(species_dev, levels, cell_count)
    gathered = lax.all_gather(own_part, "spec", axis=0, tiled=True)
    chemistry = section_chain(
        gathered,
        first_factor,
        second_factor,
        jac_used,
        lax.axis_index("spec") * species_dev,
        species_dev,
    )
    cell_index = jnp.arange(cell_count, dtype=jnp.int32)
    active_mask = cell_index[None, :] < counts[0][:, None]
    chem_wide = chemistry.astype(jnp.float32)
    adjoint_flat = adjoint.reshape(species_dev, levels, cell_count)
    adjoint_state = adjoint_flat + jnp.where(
        active_mask[None], chem_wide, jnp.zeros_like(chem_wide)
    )
    adjoint_state = adjoint_state.reshape(species_dev, levels, rows_dev, seam_len)
    upper_code = seam_codes[0, 0]
    lower_code = seam_codes[0, 1]
    seam_row = passed_along(courant[:, -1:, :], "tile", 1)
    lower_faces = jnp.concatenate([reorder(seam_row, lower_code), courant[:, :-1, :]], axis=1)
    rising = jnp.maximum(courant, 0.0)
    falling = jnp.minimum(lower_faces, 0.0)
    for substep in range(NSUB):
        extended = padded(adjoint_state.astype(jnp.bfloat16), (("tile", 2),), 1).astype(
            adjoint_state.dtype
        )
        below_rim = reorder(extended[:, :, :1, :], lower_code)
        above_rim = reorder(extended[:, :, -1:, :], upper_code)
        above_cells = jnp.concatenate([adjoint_state[:, :, 1:, :], above_rim], axis=2)
        below_cells = jnp.concatenate([below_rim, adjoint_state[:, :, :-1, :]], axis=2)
        adjoint_state = (
            adjoint_state
            + rising * (above_cells - adjoint_state)
            + falling * (adjoint_state - below_cells)
        )
    return adjoint_state


def solution(mesh):
    in_specs = (
        P("spec", None, "tile", None),
        P("tile", None, None, None),
        P("tile", None, None, None),
        P("tile", None, None, None),
        P("tile", None, None, None),
        P("tile", None),
        P(None, "tile", None),
        P("tile", None),
    )
    out_specs = P("spec", None, "tile", None)
    return jax.shard_map(shards, mesh=mesh, in_specs=in_specs, out_specs=out_specs, check_vma=False)
```

profile of v0, /device:TPU:1, one launch (start us, length us, event | category | flops | bytes accessed | tf_op | source)
XLA Modules:
  0.0 146.1 jit_solution(7802152960025787586)
XLA Ops:
  6.6 1.2 convert_element_type.91
  8.0 0.8 copy.31
  8.8 4.0 %collective-permute-start.2 = (f32[8,1,128]{2,1,0:T(1,128)S(1)}, f32[8,1,128]{2,1,0:T(1,128)S(1)}, u32[]{:S(2)}, u32[]{:S(2)}) collective-permute-start(f32[8,1,128]{2,1,0:T(1,128)S(1)} %slice.90), channel_id=1, source_target_pairs={{0,4},{4,8},{8,12},{12,16},{16,20},{20,24},{24,28},{28,32},{32,36}... | collective-permute-start | bytes 12296 | tf_op jit(solution)/shard_map/ppermute | solution.py:14
  13.5 1.0 reshape.60
  16.9 9.6 %collective-permute-done.2 = f32[8,1,128]{2,1,0:T(1,128)S(1)} collective-permute-done((f32[8,1,128]{2,1,0:T(1,128)S(1)}, f32[8,1,128]{2,1,0:T(1,128)S(1)}, u32[]{:S(2)}, u32[]{:S(2)}) %collective-permute-start.2) | collective-permute-done | bytes 4128 | tf_op jit(solution)/shard_map/ppermute | solution.py:14
  26.6 23.0 %all-gather.2.cloned.1.call-done = bf16[128,8,512]{2,0,1:T(8,128)(2,1)} async-done(((bf16[32,8,512]{2,0,1:T(8,128)(2,1)}), bf16[128,8,512]{2,0,1:T(8,128)(2,1)}) %all-gather.2.cloned.1.call-update) | async-done | bytes 1048592 | tf_op jit(solution)/shard_map/all_gather | solution.py:71
  49.6 2.7 %fusion.3 = bf16[128,8,512]{0,2,1:T(8,128)(2,1)} fusion(bf16[128,8,512]{2,0,1:T(8,128)(2,1)} %all-gather.2.cloned.1.call-done, bf16[1,8,128,128]{3,2,1,0:T(8,128)(2,1)S(1)} %copy-done), kind=kOutput, calls=%fused_computation.14 | convolution fusion | flops 134742016 | bytes 2359296 | tf_op jit(solution)/shard_map/lsp,slc->plc/dot_general | solution.py:32
  52.3 2.2 %fusion.14 = f32[8,512,128]{1,2,0:T(8,128)S(1)} fusion(bf16[8,128,128]{1,2,0:T(8,128)(2,1)} %bitcast_select_fusion, bf16[128,8,512]{0,2,1:T(8,128)(2,1)} %fusion.3, bf16[1,8,128,128]{3,2,1,0:T(8,128)(2,1)} %param.10), kind=kOutput, calls=%fused_computation.25 | convolution fusion | flops 268959744 | bytes 3670016 | tf_op jit(solution)/shard_map/lsp,slc->plc/dot_general | solution.py:32
  54.5 1.5 %fusion.5 = bf16[128,8,512]{0,2,1:T(8,128)(2,1)} fusion(bf16[128,8,512]{2,0,1:T(8,128)(2,1)S(1)} %copy-done.1, f32[8,512,128]{1,2,0:T(8,128)S(1)} %fusion.14, bf16[1,8,128,128]{3,2,1,0:T(8,128)(2,1)S(1)} %copy-done), kind=kOutput, calls=%fused_computation.16 | convolution fusion | flops 136839168 | bytes 4456448 | tf_op jit(solution)/shard_map/lsp,slc->plc/dot_general | solution.py:32
  56.0 3.4 %fusion.13 = f32[8,512,128]{1,2,0:T(8,128)} fusion(bf16[8,128,128]{1,2,0:T(8,128)(2,1)} %bitcast_select_fusion, bf16[128,8,512]{0,2,1:T(8,128)(2,1)} %fusion.5, bf16[1,8,128,128]{3,2,1,0:T(8,128)(2,1)} %param.10), kind=kOutput, calls=%fused_computation.24 | convolution fusion | flops 268959744 | bytes 3670016 | tf_op jit(solution)/shard_map/lsp,slc->plc/dot_general | solution.py:32
  59.5 3.2 %fusion.7 = bf16[128,8,512]{0,2,1:T(8,128)(2,1)} fusion(bf16[128,8,512]{2,0,1:T(8,128)(2,1)S(1)} %copy-done.1, f32[8,512,128]{1,2,0:T(8,128)} %fusion.13, bf16[1,8,128,128]{3,2,1,0:T(8,128)(2,1)S(1)} %copy-done), kind=kOutput, calls=%fused_computation.18 | convolution fusion | flops 136839168 | bytes 4456448 | tf_op jit(solution)/shard_map/lsp,slc->plc/dot_general | solution.py:32
  62.6 3.4 %fusion.12 = f32[8,512,128]{1,2,0:T(8,128)} fusion(bf16[8,128,128]{1,2,0:T(8,128)(2,1)} %bitcast_select_fusion, bf16[128,8,512]{0,2,1:T(8,128)(2,1)} %fusion.7, bf16[1,8,128,128]{3,2,1,0:T(8,128)(2,1)} %param.10), kind=kOutput, calls=%fused_computation.23 | convolution fusion | flops 268959744 | bytes 3670016 | tf_op jit(solution)/shard_map/lsp,slc->plc/dot_general | solution.py:32
  66.0 3.2 %fusion.9 = bf16[128,8,512]{0,2,1:T(8,128)(2,1)} fusion(bf16[128,8,512]{2,0,1:T(8,128)(2,1)S(1)} %copy-done.1, f32[8,512,128]{1,2,0:T(8,128)} %fusion.12, bf16[1,8,128,128]{3,2,1,0:T(8,128)(2,1)S(1)} %copy-done), kind=kOutput, calls=%fused_computation.20 | convolution fusion | flops 136839168 | bytes 4456448 | tf_op jit(solution)/shard_map/lsp,slc->plc/dot_general | solution.py:32
  69.2 2.7 %fusion.21 = f32[32,8,512]{2,0,1:T(8,128)S(1)} fusion(bf16[128,8,512]{0,2,1:T(8,128)(2,1)} %fusion.9, f32[32,8,512]{2,1,0:T(8,128)} %reshape.60, f32[8,512,128]{1,2,0:T(8,128)} %fusion.12, s32[]{:T(128)S(6)} %select_n.61, f32[8,512,128]{1,2,0:T(8,128)} %fusion.13, f32[8,512,128]{1,2,0:T(8,128)S(1)} %fusion.14, bf16[1,8,128,128]{3,2,1,0:T(8,128)(2,1)} %param.10, ...), kind=kOutput, calls=%fused_computation.32 | convolution fusion | flops 169738240 | bytes 4002816 | tf_op jit(solution)/shard_map/lsp,slc->plc/dot_general | solution.py:32
  72.3 2.2 %collective-permute-start = (bf16[32,8,1,128]{3,2,1,0:T(2,128)(2,1)S(1)}, bf16[32,8,1,128]{3,2,1,0:T(2,128)(2,1)S(1)}, u32[]{:S(2)}, u32[]{:S(2)}) collective-permute-start(bf16[32,8,1,128]{3,2,1,0:T(2,128)(2,1)S(1)} %get-tuple-element.33), channel_id=1, source_target_pairs={{0,4},{4,8},{8,12},{12,16},{16,20},{20,24},{24,28},{28,32},{32,36}... | collective-permute-start | bytes 196616 | tf_op jit(solution)/shard_map/ppermute | solution.py:23
  74.5 9.1 %collective-permute-start.1 = (bf16[32,8,1,128]{3,2,1,0:T(2,128)(2,1)S(1)}, bf16[32,8,1,128]{3,2,1,0:T(2,128)(2,1)S(1)}, u32[]{:S(2)}, u32[]{:S(2)}) collective-permute-start(bf16[32,8,1,128]{3,2,1,0:T(2,128)(2,1)S(1)} %get-tuple-element.34), channel_id=1, source_target_pairs={{4,0},{8,4},{12,8},{16,12},{20,16},{24,20},{28,24},{32,28},{36,32}... | collective-permute-start | bytes 196616 | tf_op jit(solution)/shard_map/ppermute | solution.py:26
  83.9 1.1 collective-permute-done
  85.0 0.9 collective-permute-done.1
  85.9 0.7 maximum_convert_fusion.3
  88.7 1.9 %collective-permute-start.3 = (bf16[32,8,1,128]{3,2,1,0:T(2,128)(2,1)S(1)}, bf16[32,8,1,128]{3,2,1,0:T(2,128)(2,1)S(1)}, u32[]{:S(2)}, u32[]{:S(2)}) collective-permute-start(bf16[32,8,1,128]{3,2,1,0:T(2,128)(2,1)S(1)} %get-tuple-element.31), channel_id=1, source_target_pairs={{0,4},{4,8},{8,12},{12,16},{16,20},{20,24},{24,28},{28,32},{32,36}... | collective-permute-start | bytes 196616 | tf_op jit(solution)/shard_map/ppermute | solution.py:23
  90.6 10.1 %collective-permute-start.4 = (bf16[32,8,1,128]{3,2,1,0:T(2,128)(2,1)S(1)}, bf16[32,8,1,128]{3,2,1,0:T(2,128)(2,1)S(1)}, u32[]{:S(2)}, u32[]{:S(2)}) collective-permute-start(bf16[32,8,1,128]{3,2,1,0:T(2,128)(2,1)S(1)} %get-tuple-element.32), channel_id=1, source_target_pairs={{4,0},{8,4},{12,8},{16,12},{20,16},{24,20},{28,24},{32,28},{36,32}... | collective-permute-start | bytes 196616 | tf_op jit(solution)/shard_map/ppermute | solution.py:26
  101.3 1.4 collective-permute-done.4
  102.7 0.8 maximum_convert_fusion.2
  105.5 1.9 %collective-permute-start.5 = (bf16[32,8,1,128]{3,2,1,0:T(2,128)(2,1)S(1)}, bf16[32,8,1,128]{3,2,1,0:T(2,128)(2,1)S(1)}, u32[]{:S(2)}, u32[]{:S(2)}) collective-permute-start(bf16[32,8,1,128]{3,2,1,0:T(2,128)(2,1)S(1)} %get-tuple-element.29), channel_id=1, source_target_pairs={{0,4},{4,8},{8,12},{12,16},{16,20},{20,24},{24,28},{28,32},{32,36}... | collective-permute-start | bytes 196616 | tf_op jit(solution)/shard_map/ppermute | solution.py:23
  107.5 10.1 %collective-permute-start.6 = (bf16[32,8,1,128]{3,2,1,0:T(2,128)(2,1)S(1)}, bf16[32,8,1,128]{3,2,1,0:T(2,128)(2,1)S(1)}, u32[]{:S(2)}, u32[]{:S(2)}) collective-permute-start(bf16[32,8,1,128]{3,2,1,0:T(2,128)(2,1)S(1)} %get-tuple-element.30), channel_id=1, source_target_pairs={{4,0},{8,4},{12,8},{16,12},{20,16},{24,20},{28,24},{32,28},{36,32}... | collective-permute-start | bytes 196616 | tf_op jit(solution)/shard_map/ppermute | solution.py:26
  117.9 1.4 collective-permute-done.6
  119.3 0.8 maximum_convert_fusion.1
  122.1 1.9 %collective-permute-start.7 = (bf16[32,8,1,128]{3,2,1,0:T(2,128)(2,1)S(1)}, bf16[32,8,1,128]{3,2,1,0:T(2,128)(2,1)S(1)}, u32[]{:S(2)}, u32[]{:S(2)}) collective-permute-start(bf16[32,8,1,128]{3,2,1,0:T(2,128)(2,1)S(1)} %get-tuple-element.27), channel_id=1, source_target_pairs={{0,4},{4,8},{8,12},{12,16},{16,20},{20,24},{24,28},{28,32},{32,36}... | collective-permute-start | bytes 196616 | tf_op jit(solution)/shard_map/ppermute | solution.py:23
  124.1 9.9 %collective-permute-start.8 = (bf16[32,8,1,128]{3,2,1,0:T(2,128)(2,1)S(1)}, bf16[32,8,1,128]{3,2,1,0:T(2,128)(2,1)S(1)}, u32[]{:S(2)}, u32[]{:S(2)}) collective-permute-start(bf16[32,8,1,128]{3,2,1,0:T(2,128)(2,1)S(1)} %get-tuple-element.28), channel_id=1, source_target_pairs={{4,0},{8,4},{12,8},{16,12},{20,16},{24,20},{28,24},{32,28},{36,32}... | collective-permute-start | bytes 196616 | tf_op jit(solution)/shard_map/ppermute | solution.py:26
  134.4 1.5 collective-permute-done.8
  135.9 0.8 fusion.56
  137.9 1.3 fusion.42
  (63 shorter events, 11.4 us)
Async XLA Ops:
  6.5 43.1 %copy-start = (bf16[1,8,128,128]{3,2,1,0:T(8,128)(2,1)S(1)}, bf16[1,8,128,128]{3,2,1,0:T(8,128)(2,1)}, u32[]{:S(2)}) copy-start(bf16[1,8,128,128]{3,2,1,0:T(8,128)(2,1)} %param.9) | copy-start | bytes 786436
  6.5 7.0 %copy-start.2 = (f32[32,8,4,128]{3,2,1,0:T(4,128)S(1)}, f32[32,8,4,128]{3,2,1,0:T(4,128)}, u32[]{:S(2)}) copy-start(f32[32,8,4,128]{3,2,1,0:T(4,128)} %param.8) | copy-start | bytes 1572868
  6.5 2.2 %copy-start.4 = (f32[8,4,128]{2,1,0:T(4,128)S(1)}, f32[8,4,128]{2,1,0:T(4,128)}, u32[]{:S(2)}) copy-start(f32[8,4,128]{2,1,0:T(4,128)} %param.14) | copy-start | bytes 49156
  6.5 6.3 %copy-start.5 = (s32[1,8,2,2]{1,3,2,0:T(2,128)S(1)}, s32[1,8,2,2]{1,3,2,0:T(2,128)}, u32[]{:S(2)}) copy-start(s32[1,8,2,2]{1,3,2,0:T(2,128)} %param.12) | copy-start | bytes 388
  6.5 6.3 %copy-start.7 = (s32[1,8]{1,0:T(1,128)S(1)}, s32[1,8]{1,0:T(1,128)}, u32[]{:S(2)}) copy-start(s32[1,8]{1,0:T(1,128)} %param.13) | copy-start | bytes 100
  6.5 6.4 %copy-start.6 = (s32[1,2]{1,0:T(1,128)S(1)}, s32[1,2]{1,0:T(1,128)}, u32[]{:S(2)}) copy-start(s32[1,2]{1,0:T(1,128)} %param.15) | copy-start | bytes 28
  6.6 8.0 %copy-start.3 = (bf16[1,8,128,128]{3,2,1,0:T(8,128)(2,1)S(1)}, bf16[1,8,128,128]{3,2,1,0:T(8,128)(2,1)}, u32[]{:S(2)}) copy-start(bf16[1,8,128,128]{3,2,1,0:T(8,128)(2,1)} %param.11) | copy-start | bytes 786436
  6.6 43.0 %all-gather.2.cloned.1.call-start = ((), (), s32[]{:S(2)}) async-start(), calls=%async_computation | async-start | bytes 1310720 | tf_op jit(solution)/shard_map/all_gather | solution.py:71
  8.8 17.7 %collective-permute-start.2 = (f32[8,1,128]{2,1,0:T(1,128)S(1)}, f32[8,1,128]{2,1,0:T(1,128)S(1)}, u32[]{:S(2)}, u32[]{:S(2)}) collective-permute-start(f32[8,1,128]{2,1,0:T(1,128)S(1)} %slice.90), channel_id=1, source_target_pairs={{0,4},{4,8},{8,12},{12,16},{16,20},{20,24},{24,28},{28,32},{32,36}... | collective-permute-start | bytes 12296 | tf_op jit(solution)/shard_map/ppermute | solution.py:14
  52.3 2.2 %copy-start.1 = (bf16[128,8,512]{2,0,1:T(8,128)(2,1)S(1)}, bf16[128,8,512]{2,0,1:T(8,128)(2,1)}, u32[]{:S(2)}) copy-start(bf16[128,8,512]{2,0,1:T(8,128)(2,1)} %all-gather.2.cloned.1.call-done) | copy-start | bytes 3145732
  72.3 12.7 %collective-permute-start = (bf16[32,8,1,128]{3,2,1,0:T(2,128)(2,1)S(1)}, bf16[32,8,1,128]{3,2,1,0:T(2,128)(2,1)S(1)}, u32[]{:S(2)}, u32[]{:S(2)}) collective-permute-start(bf16[32,8,1,128]{3,2,1,0:T(2,128)(2,1)S(1)} %get-tuple-element.33), channel_id=1, source_target_pairs={{0,4},{4,8},{8,12},{12,16},{16,20},{20,24},{24,28},{28,32},{32,36}... | collective-permute-start | bytes 196616 | tf_op jit(solution)/shard_map/ppermute | solution.py:23
  74.5 11.4 %collective-permute-start.1 = (bf16[32,8,1,128]{3,2,1,0:T(2,128)(2,1)S(1)}, bf16[32,8,1,128]{3,2,1,0:T(2,128)(2,1)S(1)}, u32[]{:S(2)}, u32[]{:S(2)}) collective-permute-start(bf16[32,8,1,128]{3,2,1,0:T(2,128)(2,1)S(1)} %get-tuple-element.34), channel_id=1, source_target_pairs={{4,0},{8,4},{12,8},{16,12},{20,16},{24,20},{28,24},{32,28},{36,32}... | collective-permute-start | bytes 196616 | tf_op jit(solution)/shard_map/ppermute | solution.py:26
  88.7 12.6 %collective-permute-start.3 = (bf16[32,8,1,128]{3,2,1,0:T(2,128)(2,1)S(1)}, bf16[32,8,1,128]{3,2,1,0:T(2,128)(2,1)S(1)}, u32[]{:S(2)}, u32[]{:S(2)}) collective-permute-start(bf16[32,8,1,128]{3,2,1,0:T(2,128)(2,1)S(1)} %get-tuple-element.31), channel_id=1, source_target_pairs={{0,4},{4,8},{8,12},{12,16},{16,20},{20,24},{24,28},{28,32},{32,36}... | collective-permute-start | bytes 196616 | tf_op jit(solution)/shard_map/ppermute | solution.py:23
  90.6 12.1 %collective-permute-start.4 = (bf16[32,8,1,128]{3,2,1,0:T(2,128)(2,1)S(1)}, bf16[32,8,1,128]{3,2,1,0:T(2,128)(2,1)S(1)}, u32[]{:S(2)}, u32[]{:S(2)}) collective-permute-start(bf16[32,8,1,128]{3,2,1,0:T(2,128)(2,1)S(1)} %get-tuple-element.32), channel_id=1, source_target_pairs={{4,0},{8,4},{12,8},{16,12},{20,16},{24,20},{28,24},{32,28},{36,32}... | collective-permute-start | bytes 196616 | tf_op jit(solution)/shard_map/ppermute | solution.py:26
  105.5 12.4 %collective-permute-start.5 = (bf16[32,8,1,128]{3,2,1,0:T(2,128)(2,1)S(1)}, bf16[32,8,1,128]{3,2,1,0:T(2,128)(2,1)S(1)}, u32[]{:S(2)}, u32[]{:S(2)}) collective-permute-start(bf16[32,8,1,128]{3,2,1,0:T(2,128)(2,1)S(1)} %get-tuple-element.29), channel_id=1, source_target_pairs={{0,4},{4,8},{8,12},{12,16},{16,20},{20,24},{24,28},{28,32},{32,36}... | collective-permute-start | bytes 196616 | tf_op jit(solution)/shard_map/ppermute | solution.py:23
  107.5 11.9 %collective-permute-start.6 = (bf16[32,8,1,128]{3,2,1,0:T(2,128)(2,1)S(1)}, bf16[32,8,1,128]{3,2,1,0:T(2,128)(2,1)S(1)}, u32[]{:S(2)}, u32[]{:S(2)}) collective-permute-start(bf16[32,8,1,128]{3,2,1,0:T(2,128)(2,1)S(1)} %get-tuple-element.30), channel_id=1, source_target_pairs={{4,0},{8,4},{12,8},{16,12},{20,16},{24,20},{28,24},{32,28},{36,32}... | collective-permute-start | bytes 196616 | tf_op jit(solution)/shard_map/ppermute | solution.py:26
  122.1 12.3 %collective-permute-start.7 = (bf16[32,8,1,128]{3,2,1,0:T(2,128)(2,1)S(1)}, bf16[32,8,1,128]{3,2,1,0:T(2,128)(2,1)S(1)}, u32[]{:S(2)}, u32[]{:S(2)}) collective-permute-start(bf16[32,8,1,128]{3,2,1,0:T(2,128)(2,1)S(1)} %get-tuple-element.27), channel_id=1, source_target_pairs={{0,4},{4,8},{8,12},{12,16},{16,20},{20,24},{24,28},{28,32},{32,36}... | collective-permute-start | bytes 196616 | tf_op jit(solution)/shard_map/ppermute | solution.py:23
  124.1 11.8 %collective-permute-start.8 = (bf16[32,8,1,128]{3,2,1,0:T(2,128)(2,1)S(1)}, bf16[32,8,1,128]{3,2,1,0:T(2,128)(2,1)S(1)}, u32[]{:S(2)}, u32[]{:S(2)}) collective-permute-start(bf16[32,8,1,128]{3,2,1,0:T(2,128)(2,1)S(1)} %get-tuple-element.28), channel_id=1, source_target_pairs={{4,0},{8,4},{12,8},{16,12},{20,16},{24,20},{28,24},{32,28},{36,32}... | collective-permute-start | bytes 196616 | tf_op jit(solution)/shard_map/ppermute | solution.py:26
Sparse Core Ops, SparseCore 0:
  9.5 40.0 all-gather.1
where the time goes:
time: 147 us; the launch traced here: 146 us
  starting transfers between devices  51.2 us (35%)
  waiting for transfers between devices  39.2 us (27%)
  matrix products  22.3 us (15%)
  between operations  15 us (10%)
  local copies, waits for them, and re-layouts  9.97 us (7%)
  other arithmetic  8.42 us (6%)
    ppermute x4, starting transfers between devices, padded(): lax.ppermute(lax.slice_in_dim(block, 0, width, axis=dim), axis, backward)  39.2 us
    all_gather x1, waiting for transfers between devices, shards(): gathered = lax.all_gather(own_part, 'spec', axis=0, tiled=True)  23 us
    dot_general x8, matrix products, transposed(): jnp.einsum('lsp,slc->plc', matrix, field_cells, preferred_element_type=jn...  22.3 us
    ppermute x1, waiting for transfers between devices, passed_along(): return lax.ppermute(value, axis, pairs)  9.58 us
    ppermute x4, starting transfers between devices, padded(): lax.ppermute(lax.slice_in_dim(block, block.shape[dim] - width, None, axis...  7.93 us
    ppermute x4, waiting for transfers between devices, padded(): lax.ppermute(lax.slice_in_dim(block, 0, width, axis=dim), axis, backward)  5.19 us
    rev x9, local copies, waits for them, and re-layouts, reorder(): return jnp.where(seam_code == 1, jnp.flip(rim_cells, axis=-1), rim_cells)  4.9 us
    ppermute x1, starting transfers between devices, passed_along(): return lax.ppermute(value, axis, pairs)  4.02 us
  transfers between devices with their start and end apart: 10, of which 9 were waited for; matrix products, arithmetic and copies ran while one was open for 3% of the time, Pallas kernels for 0%

commit v1 on v0

--- a/solution.py
+++ b/solution.py
@@ -68,7 +68,9 @@
     present = jnp.repeat(jnp.repeat(pattern[0], block_size, axis=1), block_size, axis=2) == 1
     jac_used = jnp.where(present, jacobian[0], jnp.zeros_like(jacobian[0]))
     own_part = adjoint.astype(jnp.bfloat16).reshape(species_dev, levels, cell_count)
-    gathered = lax.all_gather(own_part, "spec", axis=0, tiled=True)
+    gathered = jnp.concatenate(
+        lax.all_to_all(jnp.stack([own_part] * lax.axis_size("spec")), "spec", 0, 0), axis=0
+    )
     chemistry = section_chain(
         gathered,
         first_factor,

time: 147 us -> 133 us (0.905)
  the two profiles are of different devices: /device:TPU:1 before, /device:TPU:32 now
where the time goes in v1:
time: 133 us; the launch traced here: 132 us
  starting transfers between devices  62.7 us (47%)
  waiting for transfers between devices  26.6 us (20%)
  matrix products  21.7 us (16%)
  local copies, waits for them, and re-layouts  11 us (8%)
  other arithmetic  8.38 us (6%)
  between operations  1.61 us (1%)
    ppermute x4, starting transfers between devices, padded(): lax.ppermute(lax.slice_in_dim(block, 0, width, axis=dim), axis, backward)  44.2 us
    dot_general x8, matrix products, transposed(): jnp.einsum('lsp,slc->plc', matrix, field_cells, preferred_element_type=jn...  21.7 us
    ppermute x1, waiting for transfers between devices, passed_along(): return lax.ppermute(value, axis, pairs)  16.8 us
    all_to_all x1, starting transfers between devices, shards(): lax.all_to_all(jnp.stack([own_part] * lax.axis_size('spec')), 'spec', 0, 0)  8.94 us
    ppermute x4, starting transfers between devices, padded(): lax.ppermute(lax.slice_in_dim(block, block.shape[dim] - width, None, axis...  7.68 us
    rev x9, local copies, waits for them, and re-layouts, reorder(): return jnp.where(seam_code == 1, jnp.flip(rim_cells, axis=-1), rim_cells)  4.9 us
    ppermute x4, waiting for transfers between devices, padded(): lax.ppermute(lax.slice_in_dim(block, block.shape[dim] - width, None, axis...  4.32 us
    ppermute x4, waiting for transfers between devices, padded(): lax.ppermute(lax.slice_in_dim(block, 0, width, axis=dim), axis, backward)  4.3 us
  transfers between devices with their start and end apart: 10, of which 10 were waited for; matrix products, arithmetic and copies ran while one was open for 3% of the time, Pallas kernels for 0%

profile of v1, /device:TPU:32, one launch (start us, length us, event | category | flops | bytes accessed | tf_op | source)
XLA Modules:
  0.0 131.9 jit_solution(13937858685094517536)
XLA Ops:
  0.0 1.2 convert_element_type.91
  1.5 1.1 stack.3
  2.6 8.9 %all-to-all-start = ((bf16[4,32,8,512]{3,1,2,0:T(8,128)(2,1)}), bf16[4,32,8,512]{3,1,2,0:T(8,128)(2,1)S(1)}, u32[]{:S(2)}, u32[]{:S(2)}) async-start(bf16[4,32,8,512]{3,1,2,0:T(8,128)(2,1)} %stack.3), calls=%async_computation | async-start | bytes 2097152 | tf_op jit(solution)/shard_map/all_to_all | solution.py:72
  11.5 1.9 %collective-permute-start.2 = (f32[8,1,128]{2,1,0:T(1,128)S(1)}, f32[8,1,128]{2,1,0:T(1,128)S(1)}, u32[]{:S(2)}, u32[]{:S(2)}) collective-permute-start(f32[8,1,128]{2,1,0:T(1,128)S(1)} %slice.90), channel_id=1, source_target_pairs={{0,4},{4,8},{8,12},{12,16},{16,20},{20,24},{24,28},{28,32},{32,36}... | collective-permute-start | bytes 12296 | tf_op jit(solution)/shard_map/ppermute | solution.py:14
  14.1 1.0 reshape.62
  17.6 16.8 %collective-permute-done.2 = f32[8,1,128]{2,1,0:T(1,128)S(1)} collective-permute-done((f32[8,1,128]{2,1,0:T(1,128)S(1)}, f32[8,1,128]{2,1,0:T(1,128)S(1)}, u32[]{:S(2)}, u32[]{:S(2)}) %collective-permute-start.2) | collective-permute-done | bytes 4128 | tf_op jit(solution)/shard_map/ppermute | solution.py:14
  34.5 1.1 all-to-all-done
  36.2 1.6 %fusion.3 = bf16[128,8,512]{0,2,1:T(8,128)(2,1)} fusion(bf16[128,8,512]{2,1,0:T(8,128)(2,1)S(1)} %bitcast.122, bf16[1,8,128,128]{3,2,1,0:T(8,128)(2,1)S(1)} %copy-done), kind=kOutput, calls=%fused_computation.14 | convolution fusion | flops 134742016 | bytes 2359296 | tf_op jit(solution)/shard_map/lsp,slc->plc/dot_general | solution.py:32
  37.9 2.0 %fusion.14 = f32[8,512,128]{1,2,0:T(8,128)S(1)} fusion(bf16[8,128,128]{1,2,0:T(8,128)(2,1)} %bitcast_select_fusion, bf16[128,8,512]{0,2,1:T(8,128)(2,1)} %fusion.3, bf16[1,8,128,128]{3,2,1,0:T(8,128)(2,1)} %param.10), kind=kOutput, calls=%fused_computation.25 | convolution fusion | flops 268959744 | bytes 3670016 | tf_op jit(solution)/shard_map/lsp,slc->plc/dot_general | solution.py:32
  39.9 1.8 %fusion.5 = bf16[128,8,512]{0,2,1:T(8,128)(2,1)} fusion(f32[8,512,128]{1,2,0:T(8,128)S(1)} %fusion.14, bf16[128,8,512]{2,1,0:T(8,128)(2,1)S(1)} %bitcast.123, bf16[1,8,128,128]{3,2,1,0:T(8,128)(2,1)S(1)} %copy-done), kind=kOutput, calls=%fused_computation.16 | convolution fusion | flops 136839168 | bytes 4456448 | tf_op jit(solution)/shard_map/lsp,slc->plc/dot_general | solution.py:32
  41.7 3.4 %fusion.13 = f32[8,512,128]{1,2,0:T(8,128)} fusion(bf16[8,128,128]{1,2,0:T(8,128)(2,1)} %bitcast_select_fusion, bf16[128,8,512]{0,2,1:T(8,128)(2,1)} %fusion.5, bf16[1,8,128,128]{3,2,1,0:T(8,128)(2,1)} %param.10), kind=kOutput, calls=%fused_computation.24 | convolution fusion | flops 268959744 | bytes 3670016 | tf_op jit(solution)/shard_map/lsp,slc->plc/dot_general | solution.py:32
  45.1 3.4 %fusion.7 = bf16[128,8,512]{0,2,1:T(8,128)(2,1)} fusion(f32[8,512,128]{1,2,0:T(8,128)} %fusion.13, bf16[128,8,512]{2,1,0:T(8,128)(2,1)S(1)} %bitcast.124, bf16[1,8,128,128]{3,2,1,0:T(8,128)(2,1)S(1)} %copy-done), kind=kOutput, calls=%fused_computation.18 | convolution fusion | flops 136839168 | bytes 4456448 | tf_op jit(solution)/shard_map/lsp,slc->plc/dot_general | solution.py:32
  48.5 3.4 %fusion.12 = f32[8,512,128]{1,2,0:T(8,128)} fusion(bf16[8,128,128]{1,2,0:T(8,128)(2,1)} %bitcast_select_fusion, bf16[128,8,512]{0,2,1:T(8,128)(2,1)} %fusion.7, bf16[1,8,128,128]{3,2,1,0:T(8,128)(2,1)} %param.10), kind=kOutput, calls=%fused_computation.23 | convolution fusion | flops 268959744 | bytes 3670016 | tf_op jit(solution)/shard_map/lsp,slc->plc/dot_general | solution.py:32
  51.8 3.4 %fusion.9 = bf16[128,8,512]{0,2,1:T(8,128)(2,1)} fusion(f32[8,512,128]{1,2,0:T(8,128)} %fusion.12, bf16[128,8,512]{2,1,0:T(8,128)(2,1)S(1)} %bitcast.125, bf16[1,8,128,128]{3,2,1,0:T(8,128)(2,1)S(1)} %copy-done), kind=kOutput, calls=%fused_computation.20 | convolution fusion | flops 136839168 | bytes 4456448 | tf_op jit(solution)/shard_map/lsp,slc->plc/dot_general | solution.py:32
  55.2 2.7 %fusion.21 = f32[32,8,512]{2,0,1:T(8,128)S(1)} fusion(bf16[128,8,512]{0,2,1:T(8,128)(2,1)} %fusion.9, f32[32,8,512]{2,1,0:T(8,128)} %reshape.62, f32[8,512,128]{1,2,0:T(8,128)} %fusion.12, s32[]{:T(128)S(6)} %select_n.61, f32[8,512,128]{1,2,0:T(8,128)} %fusion.13, f32[8,512,128]{1,2,0:T(8,128)S(1)} %fusion.14, bf16[1,8,128,128]{3,2,1,0:T(8,128)(2,1)} %param.10, ...), kind=kOutput, calls=%fused_computation.32 | convolution fusion | flops 169738240 | bytes 4002816 | tf_op jit(solution)/shard_map/lsp,slc->plc/dot_general | solution.py:32
  58.3 1.9 %collective-permute-start = (bf16[32,8,1,128]{3,2,1,0:T(2,128)(2,1)S(1)}, bf16[32,8,1,128]{3,2,1,0:T(2,128)(2,1)S(1)}, u32[]{:S(2)}, u32[]{:S(2)}) collective-permute-start(bf16[32,8,1,128]{3,2,1,0:T(2,128)(2,1)S(1)} %get-tuple-element.33), channel_id=1, source_target_pairs={{0,4},{4,8},{8,12},{12,16},{16,20},{20,24},{24,28},{28,32},{32,36}... | collective-permute-start | bytes 196616 | tf_op jit(solution)/shard_map/ppermute | solution.py:23
  60.2 12.7 %collective-permute-start.1 = (bf16[32,8,1,128]{3,2,1,0:T(2,128)(2,1)S(1)}, bf16[32,8,1,128]{3,2,1,0:T(2,128)(2,1)S(1)}, u32[]{:S(2)}, u32[]{:S(2)}) collective-permute-start(bf16[32,8,1,128]{3,2,1,0:T(2,128)(2,1)S(1)} %get-tuple-element.34), channel_id=1, source_target_pairs={{4,0},{8,4},{12,8},{16,12},{20,16},{24,20},{28,24},{32,28},{36,32}... | collective-permute-start | bytes 196616 | tf_op jit(solution)/shard_map/ppermute | solution.py:26
  73.9 1.5 %collective-permute-done.1 = bf16[32,8,1,128]{3,2,1,0:T(2,128)(2,1)S(1)} collective-permute-done((bf16[32,8,1,128]{3,2,1,0:T(2,128)(2,1)S(1)}, bf16[32,8,1,128]{3,2,1,0:T(2,128)(2,1)S(1)}, u32[]{:S(2)}, u32[]{:S(2)}) %collective-permute-start.1) | collective-permute-done | bytes 65568 | tf_op jit(solution)/shard_map/ppermute | solution.py:26
  78.2 1.9 %collective-permute-start.3 = (bf16[32,8,1,128]{3,2,1,0:T(2,128)(2,1)S(1)}, bf16[32,8,1,128]{3,2,1,0:T(2,128)(2,1)S(1)}, u32[]{:S(2)}, u32[]{:S(2)}) collective-permute-start(bf16[32,8,1,128]{3,2,1,0:T(2,128)(2,1)S(1)} %get-tuple-element.31), channel_id=1, source_target_pairs={{0,4},{4,8},{8,12},{12,16},{16,20},{20,24},{24,28},{28,32},{32,36}... | collective-permute-start | bytes 196616 | tf_op jit(solution)/shard_map/ppermute | solution.py:23
  80.2 10.6 %collective-permute-start.4 = (bf16[32,8,1,128]{3,2,1,0:T(2,128)(2,1)S(1)}, bf16[32,8,1,128]{3,2,1,0:T(2,128)(2,1)S(1)}, u32[]{:S(2)}, u32[]{:S(2)}) collective-permute-start(bf16[32,8,1,128]{3,2,1,0:T(2,128)(2,1)S(1)} %get-tuple-element.32), channel_id=1, source_target_pairs={{4,0},{8,4},{12,8},{16,12},{20,16},{24,20},{28,24},{32,28},{36,32}... | collective-permute-start | bytes 196616 | tf_op jit(solution)/shard_map/ppermute | solution.py:26
  91.0 1.1 collective-permute-done.3
  92.1 0.9 collective-permute-done.4
  93.1 0.8 maximum_convert_fusion.2
  95.9 1.9 %collective-permute-start.5 = (bf16[32,8,1,128]{3,2,1,0:T(2,128)(2,1)S(1)}, bf16[32,8,1,128]{3,2,1,0:T(2,128)(2,1)S(1)}, u32[]{:S(2)}, u32[]{:S(2)}) collective-permute-start(bf16[32,8,1,128]{3,2,1,0:T(2,128)(2,1)S(1)} %get-tuple-element.29), channel_id=1, source_target_pairs={{0,4},{4,8},{8,12},{12,16},{16,20},{20,24},{24,28},{28,32},{32,36}... | collective-permute-start | bytes 196616 | tf_op jit(solution)/shard_map/ppermute | solution.py:23
  97.8 10.5 %collective-permute-start.6 = (bf16[32,8,1,128]{3,2,1,0:T(2,128)(2,1)S(1)}, bf16[32,8,1,128]{3,2,1,0:T(2,128)(2,1)S(1)}, u32[]{:S(2)}, u32[]{:S(2)}) collective-permute-start(bf16[32,8,1,128]{3,2,1,0:T(2,128)(2,1)S(1)} %get-tuple-element.30), channel_id=1, source_target_pairs={{4,0},{8,4},{12,8},{16,12},{20,16},{24,20},{28,24},{32,28},{36,32}... | collective-permute-start | bytes 196616 | tf_op jit(solution)/shard_map/ppermute | solution.py:26
  108.6 1.8 %collective-permute-done.5 = bf16[32,8,1,128]{3,2,1,0:T(2,128)(2,1)S(1)} collective-permute-done((bf16[32,8,1,128]{3,2,1,0:T(2,128)(2,1)S(1)}, bf16[32,8,1,128]{3,2,1,0:T(2,128)(2,1)S(1)}, u32[]{:S(2)}, u32[]{:S(2)}) %collective-permute-start.5) | collective-permute-done | bytes 65568 | tf_op jit(solution)/shard_map/ppermute | solution.py:23
  110.8 0.8 maximum_convert_fusion.1
  113.6 1.9 %collective-permute-start.7 = (bf16[32,8,1,128]{3,2,1,0:T(2,128)(2,1)S(1)}, bf16[32,8,1,128]{3,2,1,0:T(2,128)(2,1)S(1)}, u32[]{:S(2)}, u32[]{:S(2)}) collective-permute-start(bf16[32,8,1,128]{3,2,1,0:T(2,128)(2,1)S(1)} %get-tuple-element.27), channel_id=1, source_target_pairs={{0,4},{4,8},{8,12},{12,16},{16,20},{20,24},{24,28},{28,32},{32,36}... | collective-permute-start | bytes 196616 | tf_op jit(solution)/shard_map/ppermute | solution.py:23
  115.6 10.4 %collective-permute-start.8 = (bf16[32,8,1,128]{3,2,1,0:T(2,128)(2,1)S(1)}, bf16[32,8,1,128]{3,2,1,0:T(2,128)(2,1)S(1)}, u32[]{:S(2)}, u32[]{:S(2)}) collective-permute-start(bf16[32,8,1,128]{3,2,1,0:T(2,128)(2,1)S(1)} %get-tuple-element.28), channel_id=1, source_target_pairs={{4,0},{8,4},{12,8},{16,12},{20,16},{24,20},{28,24},{32,28},{36,32}... | collective-permute-start | bytes 196616 | tf_op jit(solution)/shard_map/ppermute | solution.py:26
  127.0 1.5 %collective-permute-done.8 = bf16[32,8,1,128]{3,2,1,0:T(2,128)(2,1)S(1)} collective-permute-done((bf16[32,8,1,128]{3,2,1,0:T(2,128)(2,1)S(1)}, bf16[32,8,1,128]{3,2,1,0:T(2,128)(2,1)S(1)}, u32[]{:S(2)}, u32[]{:S(2)}) %collective-permute-start.8) | collective-permute-done | bytes 65568 | tf_op jit(solution)/shard_map/ppermute | solution.py:26
  128.5 0.8 fusion.60
  130.6 1.3 %fusion.46 = f32[32,8,4,128]{3,2,1,0:T(4,128)} fusion(f32[32,8,4,128]{3,2,1,0:T(4,128)S(1)} %get-tuple-element.6, f32[32,8,1,128]{3,2,1,0:T(1,128)S(1)} %bitcast.135, f32[32,8,3,128]{3,2,1,0:T(4,128)S(1)} %get-tuple-element.14, f32[32,8,3,128]{3,2,1,0:T(4,128)S(1)} %get-tuple-element.13, f32[32,8,1,128]{3,2,1,0:T(1,128)S(1)} %bitcast.134, ...), kind=kLoop, calls=%fused_computation.61 | loop fusion | flops 1048576 | bytes 2129920 | tf_op jit(solution)/shard_map/add | solution.py:105
  (62 shorter events, 14.2 us)
Async XLA Ops:
  0.0 36.2 %copy-start = (bf16[1,8,128,128]{3,2,1,0:T(8,128)(2,1)S(1)}, bf16[1,8,128,128]{3,2,1,0:T(8,128)(2,1)}, u32[]{:S(2)}) copy-start(bf16[1,8,128,128]{3,2,1,0:T(8,128)(2,1)} %param.9) | copy-start | bytes 786436
  1.2 10.3 %copy-start.3 = (f32[8,4,128]{2,1,0:T(4,128)S(1)}, f32[8,4,128]{2,1,0:T(4,128)}, u32[]{:S(2)}) copy-start(f32[8,4,128]{2,1,0:T(4,128)} %param.14) | copy-start | bytes 49156
  1.3 12.1 %copy-start.4 = (s32[1,8,2,2]{1,3,2,0:T(2,128)S(1)}, s32[1,8,2,2]{1,3,2,0:T(2,128)}, u32[]{:S(2)}) copy-start(s32[1,8,2,2]{1,3,2,0:T(2,128)} %param.12) | copy-start | bytes 388
  1.3 12.2 %copy-start.6 = (s32[1,8]{1,0:T(1,128)S(1)}, s32[1,8]{1,0:T(1,128)}, u32[]{:S(2)}) copy-start(s32[1,8]{1,0:T(1,128)} %param.13) | copy-start | bytes 100
  1.3 12.2 %copy-start.5 = (s32[1,2]{1,0:T(1,128)S(1)}, s32[1,2]{1,0:T(1,128)}, u32[]{:S(2)}) copy-start(s32[1,2]{1,0:T(1,128)} %param.15) | copy-start | bytes 28
  1.3 12.8 %copy-start.1 = (f32[32,8,4,128]{3,2,1,0:T(4,128)S(1)}, f32[32,8,4,128]{3,2,1,0:T(4,128)}, u32[]{:S(2)}) copy-start(f32[32,8,4,128]{3,2,1,0:T(4,128)} %param.8) | copy-start | bytes 1572868
  1.4 13.7 %copy-start.2 = (bf16[1,8,128,128]{3,2,1,0:T(8,128)(2,1)S(1)}, bf16[1,8,128,128]{3,2,1,0:T(8,128)(2,1)}, u32[]{:S(2)}) copy-start(bf16[1,8,128,128]{3,2,1,0:T(8,128)(2,1)} %param.11) | copy-start | bytes 786436
  2.6 33.1 %all-to-all-start = ((bf16[4,32,8,512]{3,1,2,0:T(8,128)(2,1)}), bf16[4,32,8,512]{3,1,2,0:T(8,128)(2,1)S(1)}, u32[]{:S(2)}, u32[]{:S(2)}) async-start(bf16[4,32,8,512]{3,1,2,0:T(8,128)(2,1)} %stack.3), calls=%async_computation | async-start | bytes 2097152 | tf_op jit(solution)/shard_map/all_to_all | solution.py:72
  11.5 22.9 %collective-permute-start.2 = (f32[8,1,128]{2,1,0:T(1,128)S(1)}, f32[8,1,128]{2,1,0:T(1,128)S(1)}, u32[]{:S(2)}, u32[]{:S(2)}) collective-permute-start(f32[8,1,128]{2,1,0:T(1,128)S(1)} %slice.90), channel_id=1, source_target_pairs={{0,4},{4,8},{8,12},{12,16},{16,20},{20,24},{24,28},{28,32},{32,36}... | collective-permute-start | bytes 12296 | tf_op jit(solution)/shard_map/ppermute | solution.py:14
  58.3 15.7 %collective-permute-start = (bf16[32,8,1,128]{3,2,1,0:T(2,128)(2,1)S(1)}, bf16[32,8,1,128]{3,2,1,0:T(2,128)(2,1)S(1)}, u32[]{:S(2)}, u32[]{:S(2)}) collective-permute-start(bf16[32,8,1,128]{3,2,1,0:T(2,128)(2,1)S(1)} %get-tuple-element.33), channel_id=1, source_target_pairs={{0,4},{4,8},{8,12},{12,16},{16,20},{20,24},{24,28},{28,32},{32,36}... | collective-permute-start | bytes 196616 | tf_op jit(solution)/shard_map/ppermute | solution.py:23
  60.2 15.2 %collective-permute-start.1 = (bf16[32,8,1,128]{3,2,1,0:T(2,128)(2,1)S(1)}, bf16[32,8,1,128]{3,2,1,0:T(2,128)(2,1)S(1)}, u32[]{:S(2)}, u32[]{:S(2)}) collective-permute-start(bf16[32,8,1,128]{3,2,1,0:T(2,128)(2,1)S(1)} %get-tuple-element.34), channel_id=1, source_target_pairs={{4,0},{8,4},{12,8},{16,12},{20,16},{24,20},{28,24},{32,28},{36,32}... | collective-permute-start | bytes 196616 | tf_op jit(solution)/shard_map/ppermute | solution.py:26
  78.2 13.9 %collective-permute-start.3 = (bf16[32,8,1,128]{3,2,1,0:T(2,128)(2,1)S(1)}, bf16[32,8,1,128]{3,2,1,0:T(2,128)(2,1)S(1)}, u32[]{:S(2)}, u32[]{:S(2)}) collective-permute-start(bf16[32,8,1,128]{3,2,1,0:T(2,128)(2,1)S(1)} %get-tuple-element.31), channel_id=1, source_target_pairs={{0,4},{4,8},{8,12},{12,16},{16,20},{20,24},{24,28},{28,32},{32,36}... | collective-permute-start | bytes 196616 | tf_op jit(solution)/shard_map/ppermute | solution.py:23
  80.2 12.9 %collective-permute-start.4 = (bf16[32,8,1,128]{3,2,1,0:T(2,128)(2,1)S(1)}, bf16[32,8,1,128]{3,2,1,0:T(2,128)(2,1)S(1)}, u32[]{:S(2)}, u32[]{:S(2)}) collective-permute-start(bf16[32,8,1,128]{3,2,1,0:T(2,128)(2,1)S(1)} %get-tuple-element.32), channel_id=1, source_target_pairs={{4,0},{8,4},{12,8},{16,12},{20,16},{24,20},{28,24},{32,28},{36,32}... | collective-permute-start | bytes 196616 | tf_op jit(solution)/shard_map/ppermute | solution.py:26
  95.9 14.5 %collective-permute-start.5 = (bf16[32,8,1,128]{3,2,1,0:T(2,128)(2,1)S(1)}, bf16[32,8,1,128]{3,2,1,0:T(2,128)(2,1)S(1)}, u32[]{:S(2)}, u32[]{:S(2)}) collective-permute-start(bf16[32,8,1,128]{3,2,1,0:T(2,128)(2,1)S(1)} %get-tuple-element.29), channel_id=1, source_target_pairs={{0,4},{4,8},{8,12},{12,16},{16,20},{20,24},{24,28},{28,32},{32,36}... | collective-permute-start | bytes 196616 | tf_op jit(solution)/shard_map/ppermute | solution.py:23
  97.8 13.0 %collective-permute-start.6 = (bf16[32,8,1,128]{3,2,1,0:T(2,128)(2,1)S(1)}, bf16[32,8,1,128]{3,2,1,0:T(2,128)(2,1)S(1)}, u32[]{:S(2)}, u32[]{:S(2)}) collective-permute-start(bf16[32,8,1,128]{3,2,1,0:T(2,128)(2,1)S(1)} %get-tuple-element.30), channel_id=1, source_target_pairs={{4,0},{8,4},{12,8},{16,12},{20,16},{24,20},{28,24},{32,28},{36,32}... | collective-permute-start | bytes 196616 | tf_op jit(solution)/shard_map/ppermute | solution.py:26
  113.6 13.4 %collective-permute-start.7 = (bf16[32,8,1,128]{3,2,1,0:T(2,128)(2,1)S(1)}, bf16[32,8,1,128]{3,2,1,0:T(2,128)(2,1)S(1)}, u32[]{:S(2)}, u32[]{:S(2)}) collective-permute-start(bf16[32,8,1,128]{3,2,1,0:T(2,128)(2,1)S(1)} %get-tuple-element.27), channel_id=1, source_target_pairs={{0,4},{4,8},{8,12},{12,16},{16,20},{20,24},{24,28},{28,32},{32,36}... | collective-permute-start | bytes 196616 | tf_op jit(solution)/shard_map/ppermute | solution.py:23
  115.6 13.0 %collective-permute-start.8 = (bf16[32,8,1,128]{3,2,1,0:T(2,128)(2,1)S(1)}, bf16[32,8,1,128]{3,2,1,0:T(2,128)(2,1)S(1)}, u32[]{:S(2)}, u32[]{:S(2)}) collective-permute-start(bf16[32,8,1,128]{3,2,1,0:T(2,128)(2,1)S(1)} %get-tuple-element.28), channel_id=1, source_target_pairs={{4,0},{8,4},{12,8},{16,12},{20,16},{24,20},{28,24},{32,28},{36,32}... | collective-permute-start | bytes 196616 | tf_op jit(solution)/shard_map/ppermute | solution.py:26
